TPU v7x, 256 devices: a whole 4x4x8 slice. The times are simulated.
256 devices in a mesh: dp: 16 (over z, x_hi), tensor: 16 (over x_lo, y, core).
Axes of the slice: x: 4 (x_hi: 2, x_lo: 2; x = x_hi * 2 + x_lo), y: 4, z: 8, core: 2. Of those that a mesh axis runs over, the one named last changes fastest.
Arguments:
- inputs: bfloat16 [8192, 2304], P(('dp', 'tensor')), may hold values from -6 to 6
- out_grad: bfloat16 [8192, 2304], P(('dp', 'tensor')), may hold values from -0.59765625 to 0.59765625
- gate_pre: bfloat16 [8192, 18432], P('dp', 'tensor'), may hold values from -6 to 6
- up_pre: bfloat16 [8192, 18432], P('dp', 'tensor'), may hold values from -6 to 6
- w_down: bfloat16 [18432, 2304], P('tensor'), may hold values from -0.046875 to 0.046875
- proj_new: bfloat16 [2304, 3, 256], replicated, may hold values from -0.125 to 0.125
- proj_old: bfloat16 [2304, 3, 256], P('tensor'), may hold values from -0.125 to 0.125
- first_old: float32 [256, 3, 18432], P('dp', None, 'tensor'), may hold values from -6 to 6
- second_old: float32 [256, 3, 18432], P('dp', None, 'tensor'), may hold values from 0.1 to 10
Outputs:
- first_new: float32 [256, 3, 18432], P('dp', None, 'tensor')
- second_new: float32 [256, 3, 18432], P('dp', None, 'tensor')
All inputs are finite; a program needn't handle non-finite values.
Results may differ from a plain program's by a relative error of at most 0.0005.
Values may be sent and summed in bfloat16 or wider, within the bound.
A program may use at most 64 MiB of HBM per device.

v0:
```python
import jax
import jax.numpy as jnp
from jax import lax
from jax.sharding import PartitionSpec as P

coeff = 0.7978845608028654


def gelu_pair(gate):
    inner = coeff * (gate + 0.044715 * gate * gate * gate)
    tval = jnp.tanh(inner)
    value = 0.5 * gate * (1.0 + tval)
    slope = 0.5 * (1.0 + tval) + 0.5 * gate * (1.0 - tval * tval) * coeff * (
        1.0 + 3.0 * 0.044715 * gate * gate
    )
    return (value, slope)


def on_device(
    inputs, out_grad, gate_pre, up_pre, w_down, proj_new, proj_old, first_old, second_old
):
    width = proj_new.shape[0]
    rank = proj_new.shape[2]
    flat = proj_new.reshape(width, 3 * rank)
    in_side = flat[:, : 2 * rank]
    out_side = flat[:, 2 * rank :]
    slab = width // lax.axis_size("tensor")
    own_new = lax.dynamic_slice_in_dim(proj_new, lax.axis_index("tensor") * slab, slab, 0)
    partial_rot = jnp.einsum("dki,dkj->kij", own_new, proj_old, preferred_element_type=jnp.float32)
    rotation = lax.psum(partial_rot, "tensor")
    in_proj = jnp.dot(
        lax.all_gather(inputs, "tensor", axis=0, tiled=True),
        in_side,
        preferred_element_type=jnp.float32,
    ).astype(jnp.bfloat16)
    piece = lax.all_gather(out_grad, "tensor", axis=0, tiled=True)
    hidden_rows = lax.dot_general(
        piece, w_down, (((1,), (1,)), ((), ())), preferred_element_type=jnp.float32
    )
    out_rows = jnp.dot(piece, out_side, preferred_element_type=jnp.float32).astype(jnp.bfloat16)
    value, slope = gelu_pair(gate_pre.astype(jnp.float32))
    up_rows = up_pre.astype(jnp.float32)
    gate_grad = (hidden_rows * up_rows * slope).astype(jnp.bfloat16)
    up_grad = (hidden_rows * value).astype(jnp.bfloat16)
    hidden = (value * up_rows).astype(jnp.bfloat16)
    contract = (((0,), (0,)), ((), ()))
    low_gate = lax.dot_general(
        in_proj[:, :rank], gate_grad, contract, preferred_element_type=jnp.float32
    )
    low_up = lax.dot_general(
        in_proj[:, rank:], up_grad, contract, preferred_element_type=jnp.float32
    )
    low_down = lax.dot_general(out_rows, hidden, contract, preferred_element_type=jnp.float32)
    low_grad = jnp.stack([low_gate, low_up, low_down], axis=1)
    full_first, full_second = (
        lax.all_gather(first_old, "dp", axis=0, tiled=True),
        lax.all_gather(second_old, "dp", axis=0, tiled=True),
    )
    summed = lax.psum_scatter(low_grad, "dp", scatter_dimension=0, tiled=True)
    share = first_old.shape[0]
    rot_rows = lax.dynamic_slice_in_dim(rotation, lax.axis_index("dp") * share, share, 1)
    turned_first = jnp.einsum("kij,jkc->ikc", rot_rows, full_first, precision=lax.Precision.HIGHEST)
    turned_second = jnp.einsum(
        "kij,jkc->ikc", rot_rows * rot_rows, full_second, precision=lax.Precision.HIGHEST
    )
    first_new = 0.9 * turned_first + 0.1 * summed
    second_new = 0.999 * turned_second + 0.001 * summed * summed
    return (first_new, second_new)


def solution(mesh):
    placed = (
        P(("dp", "tensor"), None),
        P(("dp", "tensor"), None),
        P("dp", "tensor"),
        P("dp", "tensor"),
        P("tensor", None),
        P(),
        P("tensor", None, None),
        P("dp", None, "tensor"),
        P("dp", None, "tensor"),
    )
    return jax.shard_map(
        on_device,
        mesh=mesh,
        in_specs=placed,
        out_specs=(P("dp", None, "tensor"), P("dp", None, "tensor")),
        check_vma=False,
    )
```

profile of v0, /device:TPU:8, one launch (start us, length us, event | category | flops | bytes accessed | tf_op | source)
XLA Modules:
  0.0 635.6 jit_solution(3412581405455012115)
XLA Ops:
  7.2 0.0 copy-start
  7.2 0.0 all-gather.7.cloned.1.call-start
  7.2 0.7 all-gather.7.cloned.1.call-update
  7.9 0.0 all-gather.9.cloned.1.call-start
  8.0 0.7 all-gather.9.cloned.1.call-update
  8.7 0.0 all-reduce.2.cloned.1.call-start
  8.7 0.0 copy-done
  8.7 2.2 fusion.27
  10.9 0.0 all-reduce.2.cloned.1.call-update
  11.0 0.0 all-gather.11.cloned.1.call-start
  11.0 0.5 all-gather.11.cloned.1.call-update
  11.5 0.0 reduce-scatter.2.cloned.1.call-start
  11.6 5.8 copy.11
  17.4 31.7 %all-gather.7.cloned.1.call-done = bf16[512,2304]{1,0:T(8,128)(2,1)} async-done(((bf16[32,2304]{1,0:T(8,128)(2,1)}), bf16[512,2304]{1,0:T(8,128)(2,1)}) %all-gather.7.cloned.1.call-update) | async-done | bytes 2359312 | tf_op jit(solution)/shard_map/all_gather | solution.py:32
  49.2 3.8 fusion.17
  53.0 0.0 copy-start.2
  53.0 34.8 %all-gather.9.cloned.1.call-done = bf16[512,2304]{1,0:T(8,128)(2,1)} async-done(((bf16[32,2304]{1,0:T(8,128)(2,1)}), bf16[512,2304]{1,0:T(8,128)(2,1)}) %all-gather.9.cloned.1.call-update) | async-done | bytes 2359312 | tf_op jit(solution)/shard_map/all_gather | solution.py:36
  87.8 6.5 %fusion.48 = f32[512,1152]{1,0:T(8,128)S(1)} fusion(bf16[512,2304]{1,0:T(8,128)(2,1)} %all-gather.9.cloned.1.call-done, bf16[1152,2304]{1,0:T(8,128)(2,1)} %param.13), kind=kOutput, calls=%fused_computation.60 | convolution fusion | flops 2717908992 | bytes 10027008 | tf_op jit(solution)/shard_map/dot_general | solution.py:37
  94.3 0.0 copy-start.3
  94.3 1.4 copy-done.3
  95.7 0.0 copy-done.2
  95.7 1.2 convolution_bitcast_fusion.1
  96.9 4.8 convolution_bitcast_fusion
  101.7 4.3 convolution_bitcast_fusion.2
  106.0 2.1 pad_maximum_fusion
  108.1 0.0 reduce-scatter.2.cloned.1.call-update
  108.2 0.2 all-gather.5.cloned.1.call-start
  108.4 0.3 all-gather.5.cloned.1.call-update
  108.7 103.4 %all-reduce.2.cloned.1.call-done = f32[3,256,256]{2,1,0:T(8,128)} async-done(((f32[3,256,256]{2,1,0:T(8,128)}), f32[3,256,256]{2,1,0:T(8,128)}) %all-reduce.2.cloned.1.call-update) | async-done | bytes 786448 | tf_op jit(solution)/shard_map/psum | solution.py:30
  212.1 102.2 %all-gather.11.cloned.1.call-done = f32[256,3,1152]{2,0,1:T(8,128)} async-done(((f32[16,3,1152]{2,0,1:T(8,128)}), f32[256,3,1152]{2,0,1:T(8,128)}) %all-gather.11.cloned.1.call-update) | async-done | bytes 3538960 | tf_op jit(solution)/shard_map/all_gather | solution.py:57
  314.3 214.0 %reduce-scatter.2.cloned.1.call-done = f32[16,3,1152]{2,0,1:T(8,128)} async-done(((f32[256,3,1152]{2,0,1:T(8,128)}), f32[16,3,1152]{2,0,1:T(8,128)}) %reduce-scatter.2.cloned.1.call-update) | async-done | bytes 221200 | tf_op jit(solution)/shard_map/reduce_scatter | solution.py:59
  528.3 0.0 copy-start.1
  528.3 4.5 fusion.16
  532.9 91.3 %all-gather.5.cloned.1.call-done = f32[256,3,1152]{2,0,1:T(8,128)} async-done(((f32[16,3,1152]{2,0,1:T(8,128)}), f32[256,3,1152]{2,0,1:T(8,128)}) %all-gather.5.cloned.1.call-update) | async-done | bytes 3538960 | tf_op jit(solution)/shard_map/all_gather | solution.py:56
  624.2 0.0 copy-done.1
  624.2 4.5 fusion.14
Async XLA Ops:
  7.2 1.6 copy-start
  7.2 42.0 %all-gather.7.cloned.1.call-start = ((), (), s32[]{:S(2)}) async-start(), calls=%async_computation.3 | async-start | bytes 2506752 | tf_op jit(solution)/shard_map/all_gather | solution.py:32
  7.9 79.9 %all-gather.9.cloned.1.call-start = ((), (), s32[]{:S(2)}) async-start(), calls=%async_computation.4 | async-start | bytes 2506752 | tf_op jit(solution)/shard_map/all_gather | solution.py:36
  8.7 203.5 %all-reduce.2.cloned.1.call-start = ((), (), s32[]{:S(2)}) async-start(), calls=%async_computation.1 | async-start | bytes 1572864 | tf_op jit(solution)/shard_map/psum | solution.py:30
  11.0 303.4 %all-gather.11.cloned.1.call-start = ((), (), s32[]{:S(2)}) async-start(), calls=%async_computation.6 | async-start | bytes 3760128 | tf_op jit(solution)/shard_map/all_gather | solution.py:57
  11.5 516.8 %reduce-scatter.2.cloned.1.call-start = ((), (), s32[]{:S(2)}) async-start(), calls=%async_computation.5 | async-start | bytes 3760128 | tf_op jit(solution)/shard_map/reduce_scatter | solution.py:59
  53.0 42.7 %copy-start.2 = (bf16[512,1152]{1,0:T(8,128)(2,1)S(1)}, bf16[512,1152]{1,0:T(8,128)(2,1)}, u32[]{:S(2)}) copy-start(bf16[512,1152]{1,0:T(8,128)(2,1)} %param.11) | copy-start | bytes 3538948
  94.3 1.4 copy-start.3
  108.2 516.0 %all-gather.5.cloned.1.call-start = ((), (), s32[]{:S(2)}) async-start(), calls=%async_computation.2 | async-start | bytes 3760128 | tf_op jit(solution)/shard_map/all_gather | solution.py:56
  528.3 95.9 %copy-start.1 = (f32[16,3,1152]{2,0,1:T(8,128)S(1)}, f32[16,3,1152]{2,0,1:T(8,128)}, u32[]{:S(2)}) copy-start(f32[16,3,1152]{2,0,1:T(8,128)} %reduce-scatter.2.cloned.1.call-done) | copy-start | bytes 663556
Sparse Core Ops, SparseCore 0:
  9.8 39.2 all-gather.6
  51.0 36.7 all-gather.8
  90.4 121.6 all-reduce.1
  214.6 99.6 all-gather.10
  318.2 210.0 reduce-scatter.1
  530.8 93.3 all-gather.4
where the time goes:
time: 636 us
  waiting for transfers between devices  580 us (91%)
  matrix products  31.9 us (5%)
  between operations  14.2 us (2%)
  local copies, waits for them, and re-layouts  7.26 us (1%)
    reduce_scatter x1, waiting for transfers between devices, on_device(): summed = lax.psum_scatter(low_grad, 'dp', scatter_dimension=0, tiled=True)  214 us
    psum x1, waiting for transfers between devices, on_device(): rotation = lax.psum(partial_rot, 'tensor')  103 us
    all_gather x1, waiting for transfers between devices, on_device(): lax.all_gather(second_old, 'dp', axis=0, tiled=True)  102 us
    all_gather x1, waiting for transfers between devices, on_device(): lax.all_gather(first_old, 'dp', axis=0, tiled=True)  91.3 us
    all_gather x1, waiting for transfers between devices, on_device(): piece = lax.all_gather(out_grad, 'tensor', axis=0, tiled=True)  34.8 us
    all_gather x1, waiting for transfers between devices, on_device(): lax.all_gather(inputs, 'tensor', axis=0, tiled=True)  31.7 us
  transfers between devices with their start and end apart: 6, of which 6 were waited for; matrix products, arithmetic and copies ran while one was open for 6% of the time, Pallas kernels for 0%

commit v1 on v0

--- a/solution.py
+++ b/solution.py
@@ -29,7 +29,9 @@
     partial_rot = jnp.einsum("dki,dkj->kij", own_new, proj_old, preferred_element_type=jnp.float32)
     rotation = lax.psum(partial_rot, "tensor")
     in_proj = jnp.dot(
-        lax.all_gather(inputs, "tensor", axis=0, tiled=True),
+        jnp.concatenate(
+            lax.all_to_all(jnp.stack([inputs] * lax.axis_size("tensor")), "tensor", 0, 0), axis=0
+        ),
         in_side,
         preferred_element_type=jnp.float32,
     ).astype(jnp.bfloat16)

time: 636 us -> 614 us (0.965)
  waiting for transfers between devices: 580 us -> 552 us
    all_gather x1 -> x0, waiting for transfers between devices: 31.7 us -> none  [on_device(): lax.all_gather(inputs, 'tensor', axis=0, tiled=True)]
    all_to_all x0 -> x1, waiting for transfers between devices: none -> 26.4 us  [on_device(): lax.all_to_all(jnp.stack([inputs] * lax.axis_size('tensor')), 'tensor', 0...]
    all_gather x1, waiting for transfers between devices: 34.8 us -> 11.9 us  [on_device(): piece = lax.all_gather(out_grad, 'tensor', axis=0, tiled=True)]
where the time goes in v1:
time: 614 us
  waiting for transfers between devices  552 us (90%)
  matrix products  31.2 us (5%)
  between operations  13.9 us (2%)
  local copies, waits for them, and re-layouts  9.02 us (1%)
  starting transfers between devices  6.24 us (1%)
    reduce_scatter x1, waiting for transfers between devices, on_device(): summed = lax.psum_scatter(low_grad, 'dp', scatter_dimension=0, tiled=True)  214 us
    psum x1, waiting for transfers between devices, on_device(): rotation = lax.psum(partial_rot, 'tensor')  104 us
    all_gather x1, waiting for transfers between devices, on_device(): lax.all_gather(second_old, 'dp', axis=0, tiled=True)  102 us
    all_gather x1, waiting for transfers between devices, on_device(): lax.all_gather(first_old, 'dp', axis=0, tiled=True)  91.3 us
    all_to_all x1, waiting for transfers between devices, on_device(): lax.all_to_all(jnp.stack([inputs] * lax.axis_size('tensor')), 'tensor', 0...  26.4 us
  transfers between devices with their start and end apart: 6, of which 6 were waited for; matrix products, arithmetic and copies ran while one was open for 6% of the time, Pallas kernels for 0%

profile of v1, /device:TPU:8, one launch (start us, length us, event | category | flops | bytes accessed | tf_op | source)
XLA Modules:
  0.0 614.1 jit_solution(15698266077553360290)
XLA Ops:
  7.2 0.0 copy-start
  7.2 0.0 copy-start.2
  7.2 0.0 all-gather.6.cloned.1.call-start
  7.2 0.7 all-gather.6.cloned.1.call-update
  7.9 0.0 all-reduce.2.cloned.1.call-start
  8.0 0.1 copy-done
  8.1 2.2 fusion.27
  10.3 0.0 all-reduce.2.cloned.1.call-update
  10.3 0.0 all-gather.8.cloned.1.call-start
  10.4 0.7 all-gather.8.cloned.1.call-update
  11.1 0.0 copy-done.2
  11.1 1.6 stack.10
  12.7 5.9 all-to-all-start
  18.6 0.0 reduce-scatter.2.cloned.1.call-start
  18.6 5.8 copy.11
  24.5 26.4 %all-to-all-done = bf16[16,32,2304]{2,1,0:T(8,128)(2,1)S(1)} async-done(((bf16[16,32,2304]{2,1,0:T(8,128)(2,1)}), bf16[16,32,2304]{2,1,0:T(8,128)(2,1)S(1)}, u32[]{:S(2)}, u32[]{:S(2)}) %all-to-all-start) | async-done | bytes 2359328 | tf_op jit(solution)/shard_map/all_to_all | solution.py:33
  50.8 3.1 fusion.17
  53.9 0.0 copy-start.3
  54.0 11.9 %all-gather.6.cloned.1.call-done = bf16[512,2304]{1,0:T(8,128)(2,1)} async-done(((bf16[32,2304]{1,0:T(8,128)(2,1)}), bf16[512,2304]{1,0:T(8,128)(2,1)}) %all-gather.6.cloned.1.call-update) | async-done | bytes 2359312 | tf_op jit(solution)/shard_map/all_gather | solution.py:38
  65.8 6.5 %fusion.48 = f32[512,1152]{1,0:T(8,128)S(1)} fusion(bf16[512,2304]{1,0:T(8,128)(2,1)} %all-gather.6.cloned.1.call-done, bf16[1152,2304]{1,0:T(8,128)(2,1)} %param.13), kind=kOutput, calls=%fused_computation.60 | convolution fusion | flops 2717908992 | bytes 10027008 | tf_op jit(solution)/shard_map/dot_general | solution.py:39
  72.3 0.0 copy-start.4
  72.3 1.4 copy-done.4
  73.7 0.0 copy-done.3
  73.7 1.2 convolution_bitcast_fusion.1
  74.9 4.8 convolution_bitcast_fusion
  79.7 4.4 convolution_bitcast_fusion.2
  84.1 2.1 pad_maximum_fusion
  86.2 0.0 reduce-scatter.2.cloned.1.call-update
  86.2 0.2 all-gather.4.cloned.1.call-start
  86.4 0.4 all-gather.4.cloned.1.call-update
  86.8 104.0 %all-reduce.2.cloned.1.call-done = f32[3,256,256]{2,1,0:T(8,128)} async-done(((f32[3,256,256]{2,1,0:T(8,128)}), f32[3,256,256]{2,1,0:T(8,128)}) %all-reduce.2.cloned.1.call-update) | async-done | bytes 786448 | tf_op jit(solution)/shard_map/psum | solution.py:30
  190.8 102.3 %all-gather.8.cloned.1.call-done = f32[256,3,1152]{2,0,1:T(8,128)} async-done(((f32[16,3,1152]{2,0,1:T(8,128)}), f32[256,3,1152]{2,0,1:T(8,128)}) %all-gather.8.cloned.1.call-update) | async-done | bytes 3538960 | tf_op jit(solution)/shard_map/all_gather | solution.py:59
  293.1 214.0 %reduce-scatter.2.cloned.1.call-done = f32[16,3,1152]{2,0,1:T(8,128)} async-done(((f32[256,3,1152]{2,0,1:T(8,128)}), f32[16,3,1152]{2,0,1:T(8,128)}) %reduce-scatter.2.cloned.1.call-update) | async-done | bytes 221200 | tf_op jit(solution)/shard_map/reduce_scatter | solution.py:61
  507.2 0.0 copy-start.1
  507.2 4.5 fusion.16
  511.7 91.3 %all-gather.4.cloned.1.call-done = f32[256,3,1152]{2,0,1:T(8,128)} async-done(((f32[16,3,1152]{2,0,1:T(8,128)}), f32[256,3,1152]{2,0,1:T(8,128)}) %all-gather.4.cloned.1.call-update) | async-done | bytes 3538960 | tf_op jit(solution)/shard_map/all_gather | solution.py:58
  603.0 0.0 copy-done.1
  603.0 4.5 fusion.14
Async XLA Ops:
  7.2 0.9 copy-start
  7.2 3.9 copy-start.2
  7.2 58.6 %all-gather.6.cloned.1.call-start = ((), (), s32[]{:S(2)}) async-start(), calls=%async_computation.4 | async-start | bytes 2506752 | tf_op jit(solution)/shard_map/all_gather | solution.py:38
  7.9 182.9 %all-reduce.2.cloned.1.call-start = ((), (), s32[]{:S(2)}) async-start(), calls=%async_computation.2 | async-start | bytes 1572864 | tf_op jit(solution)/shard_map/psum | solution.py:30
  10.3 282.8 %all-gather.8.cloned.1.call-start = ((), (), s32[]{:S(2)}) async-start(), calls=%async_computation.6 | async-start | bytes 3760128 | tf_op jit(solution)/shard_map/all_gather | solution.py:59
  12.7 38.1 %all-to-all-start = ((bf16[16,32,2304]{2,1,0:T(8,128)(2,1)}), bf16[16,32,2304]{2,1,0:T(8,128)(2,1)S(1)}, u32[]{:S(2)}, u32[]{:S(2)}) async-start(bf16[16,32,2304]{2,1,0:T(8,128)(2,1)} %stack.10), calls=%async_computation | async-start | bytes 4718592 | tf_op jit(solution)/shard_map/all_to_all | solution.py:33
  18.6 488.6 %reduce-scatter.2.cloned.1.call-start = ((), (), s32[]{:S(2)}) async-start(), calls=%async_computation.5 | async-start | bytes 3760128 | tf_op jit(solution)/shard_map/reduce_scatter | solution.py:61
  53.9 19.7 %copy-start.3 = (bf16[512,1152]{1,0:T(8,128)(2,1)S(1)}, bf16[512,1152]{1,0:T(8,128)(2,1)}, u32[]{:S(2)}) copy-start(bf16[512,1152]{1,0:T(8,128)(2,1)} %param.11) | copy-start | bytes 3538948
  72.3 1.4 copy-start.4
  86.2 516.8 %all-gather.4.cloned.1.call-start = ((), (), s32[]{:S(2)}) async-start(), calls=%async_computation.3 | async-start | bytes 3760128 | tf_op jit(solution)/shard_map/all_gather | solution.py:58
  507.2 95.8 %copy-start.1 = (f32[16,3,1152]{2,0,1:T(8,128)S(1)}, f32[16,3,1152]{2,0,1:T(8,128)}, u32[]{:S(2)}) copy-start(f32[16,3,1152]{2,0,1:T(8,128)} %reduce-scatter.2.cloned.1.call-done) | copy-start | bytes 663556
Sparse Core Ops, SparseCore 0:
  9.8 55.9 all-gather.5
  68.4 122.3 all-reduce.1
  193.4 99.6 all-gather.7
  297.0 210.1 reduce-scatter.1
  509.6 93.3 all-gather.3

commit v2 on v0

--- a/solution.py
+++ b/solution.py
@@ -27,7 +27,7 @@
     slab = width // lax.axis_size("tensor")
     own_new = lax.dynamic_slice_in_dim(proj_new, lax.axis_index("tensor") * slab, slab, 0)
     partial_rot = jnp.einsum("dki,dkj->kij", own_new, proj_old, preferred_element_type=jnp.float32)
-    rotation = lax.psum(partial_rot, "tensor")
+    rotation = jnp.sum(lax.all_gather(partial_rot, "tensor"), axis=0)
     in_proj = jnp.dot(
         lax.all_gather(inputs, "tensor", axis=0, tiled=True),
         in_side,

time: 636 us -> 585 us (0.920)
  waiting for transfers between devices: 580 us -> 523 us
    psum x1 -> x0, waiting for transfers between devices: 103 us -> none  [on_device(): rotation = lax.psum(partial_rot, 'tensor')]
    all_gather x0 -> x1, waiting for transfers between devices: none -> 55.5 us  [on_device(): rotation = jnp.sum(lax.all_gather(partial_rot, 'tensor'), axis=0)]
    all_gather x1, waiting for transfers between devices: 102 us -> 93.3 us  [on_device(): lax.all_gather(second_old, 'dp', axis=0, tiled=True)]
  transfers between devices with their start and end apart: 6 -> 6, of which waited for: 6 -> 6; matrix products, arithmetic and copies ran while one was open for 6% -> 7% of each run, Pallas kernels for 0% -> 0%
where the time goes in v2:
time: 585 us; the launch traced here: 584 us
  waiting for transfers between devices  523 us (89%)
  matrix products  31.9 us (5%)
  between operations  14.2 us (2%)
  other arithmetic  7.58 us (1%)
  local copies, waits for them, and re-layouts  7.26 us (1%)
    reduce_scatter x1, waiting for transfers between devices, on_device(): summed = lax.psum_scatter(low_grad, 'dp', scatter_dimension=0, tiled=True)  214 us
    all_gather x1, waiting for transfers between devices, on_device(): lax.all_gather(second_old, 'dp', axis=0, tiled=True)  93.3 us
    all_gather x1, waiting for transfers between devices, on_device(): lax.all_gather(first_old, 'dp', axis=0, tiled=True)  91.4 us
    all_gather x1, waiting for transfers between devices, on_device(): rotation = jnp.sum(lax.all_gather(partial_rot, 'tensor'), axis=0)  55.5 us
    all_gather x1, waiting for transfers between devices, on_device(): piece = lax.all_gather(out_grad, 'tensor', axis=0, tiled=True)  34.8 us
    all_gather x1, waiting for transfers between devices, on_device(): lax.all_gather(inputs, 'tensor', axis=0, tiled=True)  31.7 us
  transfers between devices with their start and end apart: 6, of which 6 were waited for; matrix products, arithmetic and copies ran while one was open for 7% of the time, Pallas kernels for 0%

profile of v2, /device:TPU:8, one launch (start us, length us, event | category | flops | bytes accessed | tf_op | source)
XLA Modules:
  0.0 584.4 jit_solution(127861698887139458)
XLA Ops:
  7.2 0.0 copy-start
  7.2 0.0 all-gather.9.cloned.1.call-start
  7.2 0.7 all-gather.9.cloned.1.call-update
  7.9 0.0 all-gather.11.cloned.1.call-start
  8.0 0.7 all-gather.11.cloned.1.call-update
  8.7 0.0 all-gather.15.cloned.1.call-start
  8.7 0.0 copy-done
  8.7 2.2 fusion.27
  11.0 0.0 all-gather.15.cloned.1.call-update
  11.0 0.0 all-gather.13.cloned.1.call-start
  11.0 0.5 all-gather.13.cloned.1.call-update
  11.6 0.0 reduce-scatter.2.cloned.1.call-start
  11.6 5.8 copy.12
  17.4 31.7 %all-gather.9.cloned.1.call-done = bf16[512,2304]{1,0:T(8,128)(2,1)} async-done(((bf16[32,2304]{1,0:T(8,128)(2,1)}), bf16[512,2304]{1,0:T(8,128)(2,1)}) %all-gather.9.cloned.1.call-update) | async-done | bytes 2359312 | tf_op jit(solution)/shard_map/all_gather | solution.py:32
  49.2 3.8 fusion.17
  53.0 0.0 copy-start.2
  53.0 34.8 %all-gather.11.cloned.1.call-done = bf16[512,2304]{1,0:T(8,128)(2,1)} async-done(((bf16[32,2304]{1,0:T(8,128)(2,1)}), bf16[512,2304]{1,0:T(8,128)(2,1)}) %all-gather.11.cloned.1.call-update) | async-done | bytes 2359312 | tf_op jit(solution)/shard_map/all_gather | solution.py:36
  87.8 6.5 %fusion.48 = f32[512,1152]{1,0:T(8,128)S(1)} fusion(bf16[512,2304]{1,0:T(8,128)(2,1)} %all-gather.11.cloned.1.call-done, bf16[1152,2304]{1,0:T(8,128)(2,1)} %param.13), kind=kOutput, calls=%fused_computation.60 | convolution fusion | flops 2717908992 | bytes 10027008 | tf_op jit(solution)/shard_map/dot_general | solution.py:37
  94.3 0.0 copy-start.3
  94.3 1.4 copy-done.3
  95.7 0.0 copy-done.2
  95.7 1.2 convolution_bitcast_fusion.1
  96.9 4.8 convolution_bitcast_fusion
  101.7 4.4 convolution_bitcast_fusion.2
  106.2 2.1 pad_maximum_fusion
  108.2 0.0 reduce-scatter.2.cloned.1.call-update
  108.2 0.2 all-gather.7.cloned.1.call-start
  108.5 0.3 all-gather.7.cloned.1.call-update
  108.8 55.5 %all-gather.15.cloned.1.call-done = f32[48,256,256]{2,1,0:T(8,128)} async-done(((f32[3,256,256]{2,1,0:T(8,128)}), f32[48,256,256]{2,1,0:T(8,128)}) %all-gather.15.cloned.1.call-update) | async-done | bytes 12582928 | tf_op jit(solution)/shard_map/all_gather | solution.py:30
  164.4 5.5 reduce_sum.9
  169.9 93.3 %all-gather.13.cloned.1.call-done = f32[256,3,1152]{2,0,1:T(8,128)} async-done(((f32[16,3,1152]{2,0,1:T(8,128)}), f32[256,3,1152]{2,0,1:T(8,128)}) %all-gather.13.cloned.1.call-update) | async-done | bytes 3538960 | tf_op jit(solution)/shard_map/all_gather | solution.py:57
  263.2 214.0 %reduce-scatter.2.cloned.1.call-done = f32[16,3,1152]{2,0,1:T(8,128)} async-done(((f32[256,3,1152]{2,0,1:T(8,128)}), f32[16,3,1152]{2,0,1:T(8,128)}) %reduce-scatter.2.cloned.1.call-update) | async-done | bytes 221200 | tf_op jit(solution)/shard_map/reduce_scatter | solution.py:59
  477.2 0.0 copy-start.1
  477.2 4.5 fusion.16
  481.7 91.4 %all-gather.7.cloned.1.call-done = f32[256,3,1152]{2,0,1:T(8,128)} async-done(((f32[16,3,1152]{2,0,1:T(8,128)}), f32[256,3,1152]{2,0,1:T(8,128)}) %all-gather.7.cloned.1.call-update) | async-done | bytes 3538960 | tf_op jit(solution)/shard_map/all_gather | solution.py:56
  573.0 0.0 copy-done.1
  573.0 4.5 fusion.14
Async XLA Ops:
  7.2 1.6 copy-start
  7.2 42.0 %all-gather.9.cloned.1.call-start = ((), (), s32[]{:S(2)}) async-start(), calls=%async_computation.2 | async-start | bytes 2506752 | tf_op jit(solution)/shard_map/all_gather | solution.py:32
  7.9 79.9 %all-gather.11.cloned.1.call-start = ((), (), s32[]{:S(2)}) async-start(), calls=%async_computation.3 | async-start | bytes 2506752 | tf_op jit(solution)/shard_map/all_gather | solution.py:36
  8.7 155.7 %all-gather.15.cloned.1.call-start = ((), (), s32[]{:S(2)}) async-start(), calls=%async_computation.6 | async-start | bytes 13369344 | tf_op jit(solution)/shard_map/all_gather | solution.py:30
  11.0 252.2 %all-gather.13.cloned.1.call-start = ((), (), s32[]{:S(2)}) async-start(), calls=%async_computation.5 | async-start | bytes 3760128 | tf_op jit(solution)/shard_map/all_gather | solution.py:57
  11.6 465.6 %reduce-scatter.2.cloned.1.call-start = ((), (), s32[]{:S(2)}) async-start(), calls=%async_computation.4 | async-start | bytes 3760128 | tf_op jit(solution)/shard_map/reduce_scatter | solution.py:59
  53.0 42.7 %copy-start.2 = (bf16[512,1152]{1,0:T(8,128)(2,1)S(1)}, bf16[512,1152]{1,0:T(8,128)(2,1)}, u32[]{:S(2)}) copy-start(bf16[512,1152]{1,0:T(8,128)(2,1)} %param.11) | copy-start | bytes 3538948
  94.3 1.4 copy-start.3
  108.2 464.8 %all-gather.7.cloned.1.call-start = ((), (), s32[]{:S(2)}) async-start(), calls=%async_computation.1 | async-start | bytes 3760128 | tf_op jit(solution)/shard_map/all_gather | solution.py:56
  477.2 95.9 %copy-start.1 = (f32[16,3,1152]{2,0,1:T(8,128)S(1)}, f32[16,3,1152]{2,0,1:T(8,128)}, u32[]{:S(2)}) copy-start(f32[16,3,1152]{2,0,1:T(8,128)} %reduce-scatter.2.cloned.1.call-done) | copy-start | bytes 663556
Sparse Core Ops, SparseCore 0:
  9.8 39.2 all-gather.8
  51.0 36.7 all-gather.10
  89.7 74.6 all-gather.14
  166.8 96.3 all-gather.12
  267.0 210.0 reduce-scatter.1
  479.6 93.3 all-gather.6
